TPU v7x, 32 devices: a whole 2x2x4 slice. The times are simulated.
32 devices in a mesh: scene: 4 (over x, core), brick: 8 (over z, y).
Axes of the slice: x: 2, y: 2, z: 4, core: 2. Of those that a mesh axis runs over, the one named last changes fastest.
Arguments:
- features: bfloat16 [4, 4096, 64], P('scene', 'brick'), may hold values from -6 to 6
- cotangent: bfloat16 [4, 4096, 64], P('scene', 'brick'), may hold values from -6 to 6
- first_weight: bfloat16 [1728, 64], replicated, may hold values from -0.15625 to 0.15625
- second_weight: bfloat16 [1728, 64], replicated, may hold values from -0.15625 to 0.15625
- send_rows: int32 [4, 1024], P('scene', 'brick'), may hold values from 0 to 512, as said below
- gather_rows: int32 [4, 8000], P('scene', 'brick'), may hold values from 0 to 640, as said below
Outputs:
- output: bfloat16 [4, 4096, 64], P('scene', 'brick')
- grad_input: bfloat16 [4, 4096, 64], P('scene', 'brick')
- grad_first: float32 [1728, 64], replicated
- grad_second: float32 [1728, 64], replicated
Inputs may be any that keep to these rules, and one draw needn't show every extreme that they name: `send_rows`: entries equal to 512 are empty slots; used entries come first in each half and name voxels on the face of active bricks towards that neighbour; in every draw some pair of neighbouring indices sends all 64 rows to each other. Index 0 sends nothing down, the last index nothing up. `gather_rows`: row 640 is the zero row; inactive slots read only it; rows 512 and up read boundary rows in the order of the neighbour's send list. Every index of brick holds exactly one active brick slot, and bricks touch only bricks of the same or an adjacent index.
All inputs are finite; a program needn't handle non-finite values.
Results may differ from a plain program's by a relative error of at most 0.0059.
Values may be sent and summed in bfloat16 or wider, within the bound.
No kernel may reach another device: no remote copies, remote signals or barrier semaphores. Data moves between devices by JAX's collectives and lax.ppermute only.
A program may use at most 64 MiB of HBM per device.

v0:
```python
import jax
import jax.numpy as jnp
from jax import lax
from jax.sharding import PartitionSpec as P

EDGE = 8
VOX = 512


def extended(block, sides, width):
    for axis, dim in sides:
        count = lax.axis_size(axis)
        forward = [(i, i + 1) for i in range(count - 1)]
        backward = [(target, source) for source, target in forward]
        low = lax.ppermute(
            lax.slice_in_dim(block, block.shape[dim] - width, None, axis=dim), axis, forward
        )
        high = lax.ppermute(lax.slice_in_dim(block, 0, width, axis=dim), axis, backward)
        block = jnp.concatenate([low, block, high], axis=dim)
    return block


def silu_slope(values):
    sig = jax.nn.sigmoid(values)
    return sig * (1.0 + values * (1.0 - sig))


def outgoing_rows(values, send_list):
    zero_row = jnp.zeros((1, values.shape[1]), values.dtype)
    return jnp.take(jnp.concatenate([values, zero_row], axis=0), send_list, axis=0)


def assemble(values, arrived, gather_list, slot_width):
    zero_row = jnp.zeros((1, values.shape[1]), values.dtype)
    pool = jnp.concatenate(
        [values, arrived[:slot_width], arrived[3 * slot_width :], zero_row], axis=0
    )
    return jnp.take(pool, gather_list, axis=0).reshape(
        -1, EDGE + 2, EDGE + 2, EDGE + 2, values.shape[1]
    )


def window_rows(padded, row_off, col_off, extent):
    slabs = [
        padded[:, row_off : row_off + extent, col_off : col_off + extent, depth : depth + extent, :]
        for depth in range(3)
    ]
    return jnp.concatenate(slabs, axis=-1).reshape(-1, 3 * padded.shape[-1])


def convolve(padded, weight, extent):
    width = padded.shape[-1]
    accumulated = jnp.zeros((padded.shape[0] * extent**3, weight.shape[1]), jnp.float32)
    for row_off in range(3):
        for col_off in range(3):
            start = (row_off * 3 + col_off) * 3 * width
            accumulated = accumulated + jnp.dot(
                window_rows(padded, row_off, col_off, extent),
                weight[start : start + 3 * width],
                preferred_element_type=jnp.float32,
            )
    return accumulated


def weight_gradient(padded, delta_rows):
    pieces = []
    for row_off in range(3):
        for col_off in range(3):
            pieces.append(
                lax.dot_general(
                    window_rows(padded, row_off, col_off, EDGE),
                    delta_rows,
                    (((0,), (0,)), ((), ())),
                    preferred_element_type=jnp.float32,
                )
            )
    return jnp.concatenate(pieces, axis=0)


def flipped(weight):
    width = weight.shape[1]
    return jnp.transpose(weight.reshape(27, width, width)[::-1], (0, 2, 1)).reshape(
        27 * width, width
    )


def shards(features, cotangent, first_weight, second_weight, send_rows, gather_rows):
    local_feat = features[0]
    local_cot = cotangent[0]
    send_list = send_rows[0]
    gather_list = gather_rows[0]
    slot_width = send_list.shape[0] // 2

    def forward_pad(values):
        arrived = extended(outgoing_rows(values, send_list), (("brick", 0),), slot_width)
        return assemble(values, arrived, gather_list, slot_width)

    def delta_pad(values):
        arrived = extended(outgoing_rows(values, send_list), (("brick", 0),), slot_width)
        return assemble(values, arrived, gather_list, slot_width)

    padded_input = forward_pad(local_feat)
    first_pre = convolve(padded_input, first_weight, EDGE)
    first_act = (first_pre * jax.nn.sigmoid(first_pre)).astype(jnp.bfloat16)
    padded_act = forward_pad(first_act)
    second_pre = convolve(padded_act, second_weight, EDGE)
    output = (second_pre * jax.nn.sigmoid(second_pre)).astype(jnp.bfloat16)
    second_delta = (local_cot.astype(jnp.float32) * silu_slope(second_pre)).astype(jnp.bfloat16)
    grad_second = weight_gradient(padded_act, second_delta)
    first_back = convolve(delta_pad(second_delta), flipped(second_weight), EDGE)
    first_delta = (first_back * silu_slope(first_pre)).astype(jnp.bfloat16)
    grad_first = weight_gradient(padded_input, first_delta)
    input_back = convolve(delta_pad(first_delta), flipped(first_weight), EDGE)
    grad_input = input_back.astype(jnp.bfloat16)
    grad_first, grad_second = lax.psum((grad_first, grad_second), ("scene", "brick"))
    grad_scale = float(lax.axis_size("scene") * lax.axis_size("brick") * VOX) ** (-0.5)
    return (output[None], grad_input[None], grad_first * grad_scale, grad_second * grad_scale)


def solution(mesh):
    in_specs = (
        P("scene", "brick", None),
        P("scene", "brick", None),
        P(),
        P(),
        P("scene", "brick"),
        P("scene", "brick"),
    )
    out_specs = (P("scene", "brick", None), P("scene", "brick", None), P(), P())
    return jax.shard_map(shards, mesh=mesh, in_specs=in_specs, out_specs=out_specs, check_vma=False)
```

profile of v0, /device:TPU:0, one launch (start us, length us, event | category | flops | bytes accessed | tf_op | source)
XLA Modules:
  0.0 242.3 jit_solution(8681243821451557241)
XLA Ops:
  7.2 0.7 compare_select_fusion.1
  7.9 1.0 copy.21
  9.0 0.7 gather_fusion
  9.8 4.9 %collective-permute-start = (bf16[64,64]{1,0:T(8,128)(2,1)S(1)}, bf16[64,64]{1,0:T(8,128)(2,1)S(1)}, u32[]{:S(2)}, u32[]{:S(2)}) collective-permute-start(bf16[64,64]{1,0:T(8,128)(2,1)S(1)} %get-tuple-element.136), channel_id=1, source_target_pairs={{0,1},{1,2},{2,3},{3,4},{4,5},{5,6},{6,7},{8,9},{9,10},{10,11},{11... | collective-permute-start | bytes 24584 | tf_op jit(solution)/shard_map/ppermute | solution.py:15
  14.7 1.3 collective-permute-start.1
  17.1 1.0 fusion.27
  19.2 1.2 collective-permute-done.1
  20.5 3.3 %gather_fusion.1 = bf16[1000,64]{1,0:T(8,128)(2,1)S(1)} fusion(bf16[641,64]{1,0:T(8,128)(2,1)S(1)} %maximum_maximum_fusion, s32[1024]{0:T(1024)S(1)} %pad_clamp_fusion), kind=kCustom, calls=%fused_computation.1.clone | custom fusion | bytes 260000 | tf_op jit(solution)/shard_map/jit(_take)/gather | solution.py:38
  27.6 0.9 multiply_convert_fusion.1
  28.7 0.8 gather_fusion.2
  30.2 4.3 %collective-permute-start.2 = (bf16[64,64]{0,1:T(8,128)(2,1)S(1)}, bf16[64,64]{0,1:T(8,128)(2,1)S(1)}, u32[]{:S(2)}, u32[]{:S(2)}) collective-permute-start(bf16[64,64]{0,1:T(8,128)(2,1)S(1)} %get-tuple-element.142), channel_id=1, source_target_pairs={{0,1},{1,2},{2,3},{3,4},{4,5},{5,6},{6,7},{8,9},{9,10},{10,11},{11... | collective-permute-start | bytes 24584 | tf_op jit(solution)/shard_map/ppermute | solution.py:15
  34.6 1.3 collective-permute-start.3
  38.2 0.6 copy.31
  41.8 0.6 copy.36
  42.4 0.6 copy.37
  43.0 0.6 copy.41
  43.6 0.6 copy.42
  44.9 0.6 copy.44
  48.8 3.3 %gather_fusion.3 = bf16[1000,64]{1,0:T(8,128)(2,1)S(1)} fusion(bf16[641,64]{1,0:T(8,128)(2,1)S(1)} %copy.25, s32[1024]{0:T(1024)S(1)} %copy-done.30), kind=kCustom, calls=%fused_computation.5.clone | custom fusion | bytes 260000 | tf_op jit(solution)/shard_map/jit(_take)/gather | solution.py:38
  54.1 1.0 convolution_add_fusion.22
  55.2 1.0 convolution_add_fusion.21
  56.4 1.0 convolution_add_fusion.20
  57.5 1.0 convolution_add_fusion.19
  58.7 1.0 convolution_add_fusion.18
  59.8 1.0 convolution_add_fusion.17
  61.0 0.7 copy-done.41
  61.6 0.9 fusion.4
  64.1 0.8 gather_fusion.4
  65.7 4.5 %collective-permute-start.4 = (bf16[64,64]{0,1:T(8,128)(2,1)S(1)}, bf16[64,64]{0,1:T(8,128)(2,1)S(1)}, u32[]{:S(2)}, u32[]{:S(2)}) collective-permute-start(bf16[64,64]{0,1:T(8,128)(2,1)S(1)} %get-tuple-element.140), channel_id=1, source_target_pairs={{0,1},{1,2},{2,3},{3,4},{4,5},{5,6},{6,7},{8,9},{9,10},{10,11},{11... | collective-permute-start | bytes 24584 | tf_op jit(solution)/shard_map/ppermute | solution.py:15
  70.2 1.5 collective-permute-start.5
  71.9 0.9 concatenate.201
  72.8 3.8 %collective-permute-done.5 = bf16[64,64]{0,1:T(8,128)(2,1)S(1)} collective-permute-done((bf16[64,64]{0,1:T(8,128)(2,1)S(1)}, bf16[64,64]{0,1:T(8,128)(2,1)S(1)}, u32[]{:S(2)}, u32[]{:S(2)}) %collective-permute-start.5) | collective-permute-done | bytes 8224 | tf_op jit(solution)/shard_map/ppermute | solution.py:18
  76.9 3.3 %gather_fusion.5 = bf16[1000,64]{1,0:T(8,128)(2,1)S(1)} fusion(bf16[641,64]{1,0:T(8,128)(2,1)S(1)} %copy.28, s32[1024]{0:T(1024)S(1)} %copy-done.30), kind=kCustom, calls=%fused_computation.6.clone | custom fusion | bytes 260000 | tf_op jit(solution)/shard_map/jit(_take)/gather | solution.py:38
  81.3 0.6 copy-done.27
  83.4 0.6 copy-done.26
  90.0 0.7 copy-done.3
  92.3 0.8 gather_fusion.6
  93.3 4.8 %collective-permute-start.6 = (bf16[64,64]{0,1:T(8,128)(2,1)S(1)}, bf16[64,64]{0,1:T(8,128)(2,1)S(1)}, u32[]{:S(2)}, u32[]{:S(2)}) collective-permute-start(bf16[64,64]{0,1:T(8,128)(2,1)S(1)} %get-tuple-element.138), channel_id=1, source_target_pairs={{0,1},{1,2},{2,3},{3,4},{4,5},{5,6},{6,7},{8,9},{9,10},{10,11},{11... | collective-permute-start | bytes 24584 | tf_op jit(solution)/shard_map/ppermute | solution.py:15
  98.1 1.3 collective-permute-start.7
  99.6 0.9 concatenate.200
  100.5 3.2 %collective-permute-done.7 = bf16[64,64]{0,1:T(8,128)(2,1)S(1)} collective-permute-done((bf16[64,64]{0,1:T(8,128)(2,1)S(1)}, bf16[64,64]{0,1:T(8,128)(2,1)S(1)}, u32[]{:S(2)}, u32[]{:S(2)}) %collective-permute-start.7) | collective-permute-done | bytes 8224 | tf_op jit(solution)/shard_map/ppermute | solution.py:18
  104.0 3.3 %gather_fusion.7 = bf16[1000,64]{1,0:T(8,128)(2,1)S(1)} fusion(bf16[641,64]{1,0:T(8,128)(2,1)S(1)} %copy.40, s32[1024]{0:T(1024)S(1)} %copy-done.30), kind=kCustom, calls=%fused_computation.7.clone | custom fusion | bytes 260000 | tf_op jit(solution)/shard_map/jit(_take)/gather | solution.py:38
  108.5 0.6 copy-done.19
  110.5 0.6 copy-done.18
  116.3 0.8 fusion.3
  117.1 115.6 %all-reduce.7.cloned.1.call-done = (f32[1728,64]{0,1:T(8,128)}, f32[1728,64]{0,1:T(8,128)}) async-done(((f32[1728,64]{0,1:T(8,128)}, f32[1728,64]{0,1:T(8,128)}), (f32[1728,64]{0,1:T(8,128)}, f32[1728,64]{0,1:T(8,128)})) %all-reduce.7.cloned.1.call-update) | async-done | bytes 884752 | tf_op jit(solution)/shard_map/psum | solution.py:115
  232.7 1.9 broadcast_multiply_fusion
  234.6 0.8 broadcast_multiply_fusion.1
  (230 shorter events, 39.6 us)
Async XLA Ops:
  7.2 225.6 %all-reduce.7.cloned.1.call-start = ((), (), s32[]{:S(2)}) async-start(), calls=%async_computation | async-start | bytes 1835008 | tf_op jit(solution)/shard_map/psum | solution.py:115
  7.9 1.8 copy-start.38
  7.9 1.0 copy-start.37
  9.0 7.1 %copy-start.1 = (bf16[1728,64]{0,1:T(8,128)(2,1)S(1)}, bf16[1728,64]{0,1:T(8,128)(2,1)}, u32[]{:S(2)}) copy-start(bf16[1728,64]{0,1:T(8,128)(2,1)} %param.13) | copy-start | bytes 663556
  9.8 6.2 %copy-start.36 = (s32[1,1000]{1,0:T(1,128)S(1)}, s32[1,1000]{1,0:T(1,128)}, u32[]{:S(2)}) copy-start(s32[1,1000]{1,0:T(1,128)} %param.15) | copy-start | bytes 12004
  9.8 9.4 %collective-permute-start = (bf16[64,64]{1,0:T(8,128)(2,1)S(1)}, bf16[64,64]{1,0:T(8,128)(2,1)S(1)}, u32[]{:S(2)}, u32[]{:S(2)}) collective-permute-start(bf16[64,64]{1,0:T(8,128)(2,1)S(1)} %get-tuple-element.136), channel_id=1, source_target_pairs={{0,1},{1,2},{2,3},{3,4},{4,5},{5,6},{6,7},{8,9},{9,10},{10,11},{11... | collective-permute-start | bytes 24584 | tf_op jit(solution)/shard_map/ppermute | solution.py:15
  14.7 5.6 %collective-permute-start.1 = (bf16[64,64]{1,0:T(8,128)(2,1)S(1)}, bf16[64,64]{1,0:T(8,128)(2,1)S(1)}, u32[]{:S(2)}, u32[]{:S(2)}) collective-permute-start(bf16[64,64]{1,0:T(8,128)(2,1)S(1)} %get-tuple-element.137), channel_id=1, source_target_pairs={{1,0},{2,1},{3,2},{4,3},{5,4},{6,5},{7,6},{9,8},{10,9},{11,10},{12... | collective-permute-start | bytes 24584 | tf_op jit(solution)/shard_map/ppermute | solution.py:18
  16.1 7.8 %copy-start.34 = (pred[1000]{0:T(1024)(128)(4,1)}, pred[1000]{0:T(1024)(128)(4,1)S(1)}, u32[]{:S(2)}) copy-start(pred[1000]{0:T(1024)(128)(4,1)S(1)} %compare_and_fusion) | copy-start | bytes 3004
  17.1 1.0 copy-start
  18.1 2.4 copy-start.29
  19.2 1.4 copy-start.31
  27.6 0.9 copy-start.2
  30.2 17.8 %collective-permute-start.2 = (bf16[64,64]{0,1:T(8,128)(2,1)S(1)}, bf16[64,64]{0,1:T(8,128)(2,1)S(1)}, u32[]{:S(2)}, u32[]{:S(2)}) collective-permute-start(bf16[64,64]{0,1:T(8,128)(2,1)S(1)} %get-tuple-element.142), channel_id=1, source_target_pairs={{0,1},{1,2},{2,3},{3,4},{4,5},{5,6},{6,7},{8,9},{9,10},{10,11},{11... | collective-permute-start | bytes 24584 | tf_op jit(solution)/shard_map/ppermute | solution.py:15
  34.6 13.5 %collective-permute-start.3 = (bf16[64,64]{0,1:T(8,128)(2,1)S(1)}, bf16[64,64]{0,1:T(8,128)(2,1)S(1)}, u32[]{:S(2)}, u32[]{:S(2)}) collective-permute-start(bf16[64,64]{0,1:T(8,128)(2,1)S(1)} %get-tuple-element.143), channel_id=1, source_target_pairs={{1,0},{2,1},{3,2},{4,3},{5,4},{6,5},{7,6},{9,8},{10,9},{11,10},{12... | collective-permute-start | bytes 24584 | tf_op jit(solution)/shard_map/ppermute | solution.py:18
  35.9 0.8 copy-start.12
  36.1 1.2 copy-start.11
  37.3 0.9 copy-start.10
  37.9 0.9 copy-start.9
  38.8 0.9 copy-start.8
  39.4 0.9 copy-start.7
  40.3 0.9 copy-start.6
  40.9 0.9 copy-start.5
  48.8 3.3 %copy-start.35 = (pred[1000]{0:T(1024)(128)(4,1)S(1)}, pred[1000]{0:T(1024)(128)(4,1)}, u32[]{:S(2)}) copy-start(pred[1000]{0:T(1024)(128)(4,1)} %copy-done.34) | copy-start | bytes 3004
  60.8 0.8 copy-start.41
  65.7 7.1 %collective-permute-start.4 = (bf16[64,64]{0,1:T(8,128)(2,1)S(1)}, bf16[64,64]{0,1:T(8,128)(2,1)S(1)}, u32[]{:S(2)}, u32[]{:S(2)}) collective-permute-start(bf16[64,64]{0,1:T(8,128)(2,1)S(1)} %get-tuple-element.140), channel_id=1, source_target_pairs={{0,1},{1,2},{2,3},{3,4},{4,5},{5,6},{6,7},{8,9},{9,10},{10,11},{11... | collective-permute-start | bytes 24584 | tf_op jit(solution)/shard_map/ppermute | solution.py:15
  70.2 6.4 %collective-permute-start.5 = (bf16[64,64]{0,1:T(8,128)(2,1)S(1)}, bf16[64,64]{0,1:T(8,128)(2,1)S(1)}, u32[]{:S(2)}, u32[]{:S(2)}) collective-permute-start(bf16[64,64]{0,1:T(8,128)(2,1)S(1)} %get-tuple-element.141), channel_id=1, source_target_pairs={{1,0},{2,1},{3,2},{4,3},{5,4},{6,5},{7,6},{9,8},{10,9},{11,10},{12... | collective-permute-start | bytes 24584 | tf_op jit(solution)/shard_map/ppermute | solution.py:18
  81.2 0.8 copy-start.27
  83.2 0.8 copy-start.26
  84.0 0.8 copy-start.25
  84.8 0.8 copy-start.24
  85.6 0.8 copy-start.23
  86.4 0.8 copy-start.22
  87.2 0.8 copy-start.21
  88.0 0.8 copy-start.20
  88.8 0.8 copy-start.33
  88.8 0.9 copy-start.43
  89.8 0.9 copy-start.3
  93.3 7.2 %collective-permute-start.6 = (bf16[64,64]{0,1:T(8,128)(2,1)S(1)}, bf16[64,64]{0,1:T(8,128)(2,1)S(1)}, u32[]{:S(2)}, u32[]{:S(2)}) collective-permute-start(bf16[64,64]{0,1:T(8,128)(2,1)S(1)} %get-tuple-element.138), channel_id=1, source_target_pairs={{0,1},{1,2},{2,3},{3,4},{4,5},{5,6},{6,7},{8,9},{9,10},{10,11},{11... | collective-permute-start | bytes 24584 | tf_op jit(solution)/shard_map/ppermute | solution.py:15
  98.1 5.6 %collective-permute-start.7 = (bf16[64,64]{0,1:T(8,128)(2,1)S(1)}, bf16[64,64]{0,1:T(8,128)(2,1)S(1)}, u32[]{:S(2)}, u32[]{:S(2)}) collective-permute-start(bf16[64,64]{0,1:T(8,128)(2,1)S(1)} %get-tuple-element.139), channel_id=1, source_target_pairs={{1,0},{2,1},{3,2},{4,3},{5,4},{6,5},{7,6},{9,8},{10,9},{11,10},{12... | collective-permute-start | bytes 24584 | tf_op jit(solution)/shard_map/ppermute | solution.py:18
  108.4 0.8 copy-start.19
  110.3 0.8 copy-start.18
  111.1 0.8 copy-start.17
  111.9 0.8 copy-start.16
  112.7 0.8 copy-start.15
  113.5 0.8 copy-start.14
  114.3 0.8 copy-start.13
  115.5 0.8 copy-start.28
  232.7 1.9 copy-start.4
  (5 other events, 3.4 us)
Sparse Core Ops, SparseCore 0:
  100.7 132.0 all-reduce.6
where the time goes:
time: 244 us; the launch traced here: 242 us
  waiting for transfers between devices  124 us (51%)
  local copies, waits for them, and re-layouts  52.4 us (21%)
  starting transfers between devices  23.9 us (10%)
  matrix products  17.2 us (7%)
  between operations  15 us (6%)
  other arithmetic  9.84 us (4%)
    psum x1, waiting for transfers between devices, shards(): lax.psum((grad_first, grad_second), ('scene', 'brick'))  116 us
    ppermute x4, starting transfers between devices, extended(): lax.ppermute(lax.slice_in_dim(block, block.shape[dim] - width, None, axis...  18.6 us
    unnamed x92, local copies, waits for them, and re-layouts  16.1 us
    dot_general x36, matrix products, convolve(): jnp.dot(window_rows(padded, row_off, col_off, extent), weight[start:start...  14.1 us
    gather x4, local copies, waits for them, and re-layouts, assemble(): jnp.take(pool, gather_list, axis=0)  13.3 us
    slice x20, local copies, waits for them, and re-layouts, convolve(): weight[start:start + 3 * width]  11.8 us
    ppermute x4, waiting for transfers between devices, extended(): lax.ppermute(lax.slice_in_dim(block, 0, width, axis=dim), axis, backward)  8.2 us
    ppermute x4, starting transfers between devices, extended(): lax.ppermute(lax.slice_in_dim(block, 0, width, axis=dim), axis, backward)  5.35 us
  transfers between devices with their start and end apart: 9, of which 4 were waited for; matrix products, arithmetic and copies ran while one was open for 10% of the time, Pallas kernels for 0%

commit v1 on v0

--- a/solution.py
+++ b/solution.py
@@ -112,7 +112,7 @@
     grad_first = weight_gradient(padded_input, first_delta)
     input_back = convolve(delta_pad(first_delta), flipped(first_weight), EDGE)
     grad_input = input_back.astype(jnp.bfloat16)
-    grad_first, grad_second = lax.psum((grad_first, grad_second), ("scene", "brick"))
+    grad_first, grad_second = lax.psum(lax.psum((grad_first, grad_second), "brick"), "scene")
     grad_scale = float(lax.axis_size("scene") * lax.axis_size("brick") * VOX) ** (-0.5)
     return (output[None], grad_input[None], grad_first * grad_scale, grad_second * grad_scale)
 

time: 244 us -> 227 us (0.930)
  waiting for transfers between devices: 124 us -> 107 us
    psum x1 -> x2, waiting for transfers between devices: 116 us -> 98.5 us  [the longest x1 63.2 us: shards(): lax.psum((grad_first, grad_second), 'brick')]
  transfers between devices with their start and end apart: 9 -> 10, of which waited for: 4 -> 5; matrix products, arithmetic and copies ran while one was open for 10% -> 11% of each run, Pallas kernels for 0% -> 0%
where the time goes in v1:
time: 227 us; the launch traced here: 225 us
  waiting for transfers between devices  107 us (47%)
  local copies, waits for them, and re-layouts  52.2 us (23%)
  starting transfers between devices  24 us (11%)
  matrix products  17.2 us (8%)
  between operations  15.1 us (7%)
  other arithmetic  9.83 us (4%)
    psum x1, waiting for transfers between devices, shards(): lax.psum((grad_first, grad_second), 'brick')  63.2 us
    psum x1, waiting for transfers between devices, shards(): lax.psum(lax.psum((grad_first, grad_second), 'brick'), 'scene')  35.3 us
    ppermute x4, starting transfers between devices, extended(): lax.ppermute(lax.slice_in_dim(block, block.shape[dim] - width, None, axis...  18.6 us
    unnamed x92, local copies, waits for them, and re-layouts  15.9 us
    dot_general x36, matrix products, convolve(): jnp.dot(window_rows(padded, row_off, col_off, extent), weight[start:start...  14.1 us
    gather x4, local copies, waits for them, and re-layouts, assemble(): jnp.take(pool, gather_list, axis=0)  13.3 us
    slice x20, local copies, waits for them, and re-layouts, convolve(): weight[start:start + 3 * width]  11.9 us
    ppermute x4, waiting for transfers between devices, extended(): lax.ppermute(lax.slice_in_dim(block, 0, width, axis=dim), axis, backward)  8.13 us
  transfers between devices with their start and end apart: 10, of which 5 were waited for; matrix products, arithmetic and copies ran while one was open for 11% of the time, Pallas kernels for 0%

profile of v1, /device:TPU:0, one launch (start us, length us, event | category | flops | bytes accessed | tf_op | source)
XLA Modules:
  0.0 225.0 jit_solution(6703782276032852042)
XLA Ops:
  7.2 0.7 compare_select_fusion.1
  7.9 1.0 copy.21
  9.0 0.7 gather_fusion
  9.8 4.9 %collective-permute-start = (bf16[64,64]{1,0:T(8,128)(2,1)S(1)}, bf16[64,64]{1,0:T(8,128)(2,1)S(1)}, u32[]{:S(2)}, u32[]{:S(2)}) collective-permute-start(bf16[64,64]{1,0:T(8,128)(2,1)S(1)} %get-tuple-element.138), channel_id=1, source_target_pairs={{0,1},{1,2},{2,3},{3,4},{4,5},{5,6},{6,7},{8,9},{9,10},{10,11},{11... | collective-permute-start | bytes 24584 | tf_op jit(solution)/shard_map/ppermute | solution.py:15
  14.7 1.3 collective-permute-start.1
  17.1 1.0 fusion.27
  19.2 1.2 collective-permute-done.1
  20.5 3.3 %gather_fusion.1 = bf16[1000,64]{1,0:T(8,128)(2,1)S(1)} fusion(bf16[641,64]{1,0:T(8,128)(2,1)S(1)} %maximum_maximum_fusion, s32[1024]{0:T(1024)S(1)} %pad_clamp_fusion), kind=kCustom, calls=%fused_computation.1.clone | custom fusion | bytes 260000 | tf_op jit(solution)/shard_map/jit(_take)/gather | solution.py:38
  27.6 0.9 multiply_convert_fusion.1
  28.7 0.8 gather_fusion.2
  30.1 4.3 %collective-permute-start.2 = (bf16[64,64]{0,1:T(8,128)(2,1)S(1)}, bf16[64,64]{0,1:T(8,128)(2,1)S(1)}, u32[]{:S(2)}, u32[]{:S(2)}) collective-permute-start(bf16[64,64]{0,1:T(8,128)(2,1)S(1)} %get-tuple-element.144), channel_id=1, source_target_pairs={{0,1},{1,2},{2,3},{3,4},{4,5},{5,6},{6,7},{8,9},{9,10},{10,11},{11... | collective-permute-start | bytes 24584 | tf_op jit(solution)/shard_map/ppermute | solution.py:15
  34.5 1.3 collective-permute-start.3
  41.7 0.6 copy.36
  44.2 0.6 copy.43
  44.8 0.6 copy.44
  46.0 0.6 copy.46
  48.7 3.3 %gather_fusion.3 = bf16[1000,64]{1,0:T(8,128)(2,1)S(1)} fusion(bf16[641,64]{1,0:T(8,128)(2,1)S(1)} %copy.25, s32[1024]{0:T(1024)S(1)} %copy-done.30), kind=kCustom, calls=%fused_computation.5.clone | custom fusion | bytes 260000 | tf_op jit(solution)/shard_map/jit(_take)/gather | solution.py:38
  54.0 1.0 convolution_add_fusion.22
  55.1 1.0 convolution_add_fusion.21
  56.3 1.0 convolution_add_fusion.20
  57.4 1.0 convolution_add_fusion.19
  58.6 1.0 convolution_add_fusion.18
  59.7 1.0 convolution_add_fusion.17
  60.9 0.7 copy-done.41
  61.5 0.9 fusion.4
  64.0 0.8 gather_fusion.4
  65.5 4.5 %collective-permute-start.4 = (bf16[64,64]{0,1:T(8,128)(2,1)S(1)}, bf16[64,64]{0,1:T(8,128)(2,1)S(1)}, u32[]{:S(2)}, u32[]{:S(2)}) collective-permute-start(bf16[64,64]{0,1:T(8,128)(2,1)S(1)} %get-tuple-element.142), channel_id=1, source_target_pairs={{0,1},{1,2},{2,3},{3,4},{4,5},{5,6},{6,7},{8,9},{9,10},{10,11},{11... | collective-permute-start | bytes 24584 | tf_op jit(solution)/shard_map/ppermute | solution.py:15
  70.0 1.5 collective-permute-start.5
  71.7 0.9 concatenate.201
  72.6 3.8 %collective-permute-done.5 = bf16[64,64]{0,1:T(8,128)(2,1)S(1)} collective-permute-done((bf16[64,64]{0,1:T(8,128)(2,1)S(1)}, bf16[64,64]{0,1:T(8,128)(2,1)S(1)}, u32[]{:S(2)}, u32[]{:S(2)}) %collective-permute-start.5) | collective-permute-done | bytes 8224 | tf_op jit(solution)/shard_map/ppermute | solution.py:18
  76.7 3.3 %gather_fusion.5 = bf16[1000,64]{1,0:T(8,128)(2,1)S(1)} fusion(bf16[641,64]{1,0:T(8,128)(2,1)S(1)} %copy.28, s32[1024]{0:T(1024)S(1)} %copy-done.30), kind=kCustom, calls=%fused_computation.6.clone | custom fusion | bytes 260000 | tf_op jit(solution)/shard_map/jit(_take)/gather | solution.py:38
  81.1 0.6 copy-done.27
  83.2 0.6 copy-done.26
  89.8 0.7 copy-done.3
  92.1 0.8 gather_fusion.6
  93.1 4.8 %collective-permute-start.6 = (bf16[64,64]{0,1:T(8,128)(2,1)S(1)}, bf16[64,64]{0,1:T(8,128)(2,1)S(1)}, u32[]{:S(2)}, u32[]{:S(2)}) collective-permute-start(bf16[64,64]{0,1:T(8,128)(2,1)S(1)} %get-tuple-element.140), channel_id=1, source_target_pairs={{0,1},{1,2},{2,3},{3,4},{4,5},{5,6},{6,7},{8,9},{9,10},{10,11},{11... | collective-permute-start | bytes 24584 | tf_op jit(solution)/shard_map/ppermute | solution.py:15
  97.9 1.3 collective-permute-start.7
  99.4 0.9 concatenate.200
  100.4 3.2 %collective-permute-done.7 = bf16[64,64]{0,1:T(8,128)(2,1)S(1)} collective-permute-done((bf16[64,64]{0,1:T(8,128)(2,1)S(1)}, bf16[64,64]{0,1:T(8,128)(2,1)S(1)}, u32[]{:S(2)}, u32[]{:S(2)}) %collective-permute-start.7) | collective-permute-done | bytes 8224 | tf_op jit(solution)/shard_map/ppermute | solution.py:18
  103.8 3.3 %gather_fusion.7 = bf16[1000,64]{1,0:T(8,128)(2,1)S(1)} fusion(bf16[641,64]{1,0:T(8,128)(2,1)S(1)} %copy.40, s32[1024]{0:T(1024)S(1)} %copy-done.30), kind=kCustom, calls=%fused_computation.7.clone | custom fusion | bytes 260000 | tf_op jit(solution)/shard_map/jit(_take)/gather | solution.py:38
  108.3 0.6 copy-done.19
  109.9 0.6 copy-done.18
  112.7 0.6 copy-done.15
  115.1 63.2 %all-reduce.9.cloned.1.call-done = (f32[1728,64]{0,1:T(8,128)}, f32[1728,64]{0,1:T(8,128)}) async-done(((f32[1728,64]{0,1:T(8,128)}, f32[1728,64]{0,1:T(8,128)}), (f32[1728,64]{0,1:T(8,128)}, f32[1728,64]{0,1:T(8,128)})) %all-reduce.9.cloned.1.call-update) | async-done | bytes 884752 | tf_op jit(solution)/shard_map/psum | solution.py:115
  179.3 0.8 fusion.3
  180.2 35.3 %all-reduce.11.cloned.1.call-done = (f32[1728,64]{0,1:T(8,128)}, f32[1728,64]{0,1:T(8,128)}) async-done(((f32[1728,64]{0,1:T(8,128)}, f32[1728,64]{0,1:T(8,128)}), (f32[1728,64]{0,1:T(8,128)}, f32[1728,64]{0,1:T(8,128)})) %all-reduce.11.cloned.1.call-update) | async-done | bytes 884752 | tf_op jit(solution)/shard_map/psum | solution.py:115
  215.5 1.9 broadcast_multiply_fusion
  217.4 0.8 broadcast_multiply_fusion.1
  (233 shorter events, 40.1 us)
Async XLA Ops:
  7.2 171.2 %all-reduce.9.cloned.1.call-start = ((), (), s32[]{:S(2)}) async-start(), calls=%async_computation | async-start | bytes 1835008 | tf_op jit(solution)/shard_map/psum | solution.py:115
  7.9 1.8 copy-start.38
  7.9 1.0 copy-start.37
  9.0 7.1 %copy-start.1 = (bf16[1728,64]{0,1:T(8,128)(2,1)S(1)}, bf16[1728,64]{0,1:T(8,128)(2,1)}, u32[]{:S(2)}) copy-start(bf16[1728,64]{0,1:T(8,128)(2,1)} %param.13) | copy-start | bytes 663556
  9.8 6.2 %copy-start.36 = (s32[1,1000]{1,0:T(1,128)S(1)}, s32[1,1000]{1,0:T(1,128)}, u32[]{:S(2)}) copy-start(s32[1,1000]{1,0:T(1,128)} %param.15) | copy-start | bytes 12004
  9.8 9.4 %collective-permute-start = (bf16[64,64]{1,0:T(8,128)(2,1)S(1)}, bf16[64,64]{1,0:T(8,128)(2,1)S(1)}, u32[]{:S(2)}, u32[]{:S(2)}) collective-permute-start(bf16[64,64]{1,0:T(8,128)(2,1)S(1)} %get-tuple-element.138), channel_id=1, source_target_pairs={{0,1},{1,2},{2,3},{3,4},{4,5},{5,6},{6,7},{8,9},{9,10},{10,11},{11... | collective-permute-start | bytes 24584 | tf_op jit(solution)/shard_map/ppermute | solution.py:15
  14.7 5.6 %collective-permute-start.1 = (bf16[64,64]{1,0:T(8,128)(2,1)S(1)}, bf16[64,64]{1,0:T(8,128)(2,1)S(1)}, u32[]{:S(2)}, u32[]{:S(2)}) collective-permute-start(bf16[64,64]{1,0:T(8,128)(2,1)S(1)} %get-tuple-element.139), channel_id=1, source_target_pairs={{1,0},{2,1},{3,2},{4,3},{5,4},{6,5},{7,6},{9,8},{10,9},{11,10},{12... | collective-permute-start | bytes 24584 | tf_op jit(solution)/shard_map/ppermute | solution.py:18
  16.1 7.8 %copy-start.34 = (pred[1000]{0:T(1024)(128)(4,1)}, pred[1000]{0:T(1024)(128)(4,1)S(1)}, u32[]{:S(2)}) copy-start(pred[1000]{0:T(1024)(128)(4,1)S(1)} %compare_and_fusion) | copy-start | bytes 3004
  17.1 1.0 copy-start
  18.1 2.4 %copy-start.29 = (s32[1024]{0:T(1024)}, s32[1024]{0:T(1024)S(1)}, u32[]{:S(2)}) copy-start(s32[1024]{0:T(1024)S(1)} %pad_clamp_fusion) | copy-start | bytes 12292
  19.2 1.4 copy-start.31
  27.6 0.9 copy-start.2
  30.1 17.8 %collective-permute-start.2 = (bf16[64,64]{0,1:T(8,128)(2,1)S(1)}, bf16[64,64]{0,1:T(8,128)(2,1)S(1)}, u32[]{:S(2)}, u32[]{:S(2)}) collective-permute-start(bf16[64,64]{0,1:T(8,128)(2,1)S(1)} %get-tuple-element.144), channel_id=1, source_target_pairs={{0,1},{1,2},{2,3},{3,4},{4,5},{5,6},{6,7},{8,9},{9,10},{10,11},{11... | collective-permute-start | bytes 24584 | tf_op jit(solution)/shard_map/ppermute | solution.py:15
  34.5 13.5 %collective-permute-start.3 = (bf16[64,64]{0,1:T(8,128)(2,1)S(1)}, bf16[64,64]{0,1:T(8,128)(2,1)S(1)}, u32[]{:S(2)}, u32[]{:S(2)}) collective-permute-start(bf16[64,64]{0,1:T(8,128)(2,1)S(1)} %get-tuple-element.145), channel_id=1, source_target_pairs={{1,0},{2,1},{3,2},{4,3},{5,4},{6,5},{7,6},{9,8},{10,9},{11,10},{12... | collective-permute-start | bytes 24584 | tf_op jit(solution)/shard_map/ppermute | solution.py:18
  35.8 0.8 copy-start.12
  36.0 1.2 copy-start.11
  37.2 0.9 copy-start.10
  37.9 0.9 copy-start.9
  38.7 0.9 copy-start.8
  39.3 0.9 copy-start.7
  40.2 0.9 copy-start.6
  40.8 0.9 copy-start.5
  48.7 3.3 %copy-start.35 = (pred[1000]{0:T(1024)(128)(4,1)S(1)}, pred[1000]{0:T(1024)(128)(4,1)}, u32[]{:S(2)}) copy-start(pred[1000]{0:T(1024)(128)(4,1)} %copy-done.34) | copy-start | bytes 3004
  60.7 0.8 copy-start.41
  65.5 7.1 %collective-permute-start.4 = (bf16[64,64]{0,1:T(8,128)(2,1)S(1)}, bf16[64,64]{0,1:T(8,128)(2,1)S(1)}, u32[]{:S(2)}, u32[]{:S(2)}) collective-permute-start(bf16[64,64]{0,1:T(8,128)(2,1)S(1)} %get-tuple-element.142), channel_id=1, source_target_pairs={{0,1},{1,2},{2,3},{3,4},{4,5},{5,6},{6,7},{8,9},{9,10},{10,11},{11... | collective-permute-start | bytes 24584 | tf_op jit(solution)/shard_map/ppermute | solution.py:15
  70.0 6.4 %collective-permute-start.5 = (bf16[64,64]{0,1:T(8,128)(2,1)S(1)}, bf16[64,64]{0,1:T(8,128)(2,1)S(1)}, u32[]{:S(2)}, u32[]{:S(2)}) collective-permute-start(bf16[64,64]{0,1:T(8,128)(2,1)S(1)} %get-tuple-element.143), channel_id=1, source_target_pairs={{1,0},{2,1},{3,2},{4,3},{5,4},{6,5},{7,6},{9,8},{10,9},{11,10},{12... | collective-permute-start | bytes 24584 | tf_op jit(solution)/shard_map/ppermute | solution.py:18
  81.0 0.8 copy-start.27
  83.0 0.8 copy-start.26
  83.8 0.8 copy-start.25
  84.6 0.8 copy-start.24
  85.4 0.8 copy-start.23
  86.2 0.8 copy-start.22
  87.0 0.8 copy-start.21
  87.8 0.8 copy-start.20
  88.6 0.8 copy-start.33
  88.6 0.9 copy-start.43
  89.6 0.9 copy-start.3
  93.1 7.3 %collective-permute-start.6 = (bf16[64,64]{0,1:T(8,128)(2,1)S(1)}, bf16[64,64]{0,1:T(8,128)(2,1)S(1)}, u32[]{:S(2)}, u32[]{:S(2)}) collective-permute-start(bf16[64,64]{0,1:T(8,128)(2,1)S(1)} %get-tuple-element.140), channel_id=1, source_target_pairs={{0,1},{1,2},{2,3},{3,4},{4,5},{5,6},{6,7},{8,9},{9,10},{10,11},{11... | collective-permute-start | bytes 24584 | tf_op jit(solution)/shard_map/ppermute | solution.py:15
  97.9 5.6 %collective-permute-start.7 = (bf16[64,64]{0,1:T(8,128)(2,1)S(1)}, bf16[64,64]{0,1:T(8,128)(2,1)S(1)}, u32[]{:S(2)}, u32[]{:S(2)}) collective-permute-start(bf16[64,64]{0,1:T(8,128)(2,1)S(1)} %get-tuple-element.141), channel_id=1, source_target_pairs={{1,0},{2,1},{3,2},{4,3},{5,4},{6,5},{7,6},{9,8},{10,9},{11,10},{12... | collective-permute-start | bytes 24584 | tf_op jit(solution)/shard_map/ppermute | solution.py:18
  100.3 115.2 %all-reduce.11.cloned.1.call-start = ((), (), s32[]{:S(2)}) async-start(), calls=%async_computation.1 | async-start | bytes 1835008 | tf_op jit(solution)/shard_map/psum | solution.py:115
  108.1 0.8 copy-start.19
  109.8 0.8 copy-start.18
  110.6 0.8 copy-start.17
  112.5 0.8 copy-start.15
  113.3 0.8 copy-start.14
  114.1 0.8 copy-start.13
  178.5 0.8 copy-start.28
  215.5 1.9 copy-start.4
  (6 other events, 4.0 us)
Sparse Core Ops, SparseCore 0:
  100.4 77.8 all-reduce.8
  180.8 34.6 all-reduce.10
